TPU v7x, 256 devices: a whole 4x4x8 slice. The times are simulated.
256 devices in a mesh: section: 4 (over x), seq: 32 (over z, y), mp: 2 (over core).
Axes of the slice: x: 4, y: 4, z: 8, core: 2. Of those that a mesh axis runs over, the one named last changes fastest.
Arguments:
- text_embed: bfloat16 [320, 8192], P(None, ('seq', 'mp')), may hold values from -6 to 6
- patch_hidden: bfloat16 [256, 5120], P(('section', 'seq', 'mp')), may hold values from -8 to 8
- merge_weight: bfloat16 [5120, 8192], P(None, ('seq', 'mp')), may hold values from -0.078125 to 0.078125
- merge_bias: bfloat16 [8192], P(('seq', 'mp')), may hold values from -3 to 3
- norm_gain: bfloat16 [4, 8192], P('section'), may hold values from 0.5 to 1.5
- query_weight: bfloat16 [4, 8192, 8192], P('section', None, ('seq', 'mp')), may hold values from -0.62285876 to 0.62285876
- key_weight: bfloat16 [4, 8192, 1024], P('section', None, ('seq', 'mp')), may hold values from -0.62285876 to 0.62285876
- value_weight: bfloat16 [4, 8192, 1024], P('section', None, ('seq', 'mp')), may hold values from -0.055242717 to 0.055242717
- image_counts: int32 [2, 4], replicated, may hold values from 1 to 64, 128 in all within a row
- text_counts: int32 [2, 4], replicated, may hold values from 1 to 16, 32 in all within a row
Outputs:
- hidden_states: bfloat16 [4, 320, 8192], P('section', None, ('seq', 'mp'))
Inputs may be any that keep to these rules, and one draw needn't show every extreme that they name: `image_counts`: each micro-batch's image counts sum to 256 / 2. `text_counts`: each micro-batch's image and text counts together sum to 160.
All inputs are finite; a program needn't handle non-finite values.
Results may differ from a plain program's by a relative error of at most 0.017.
Values may be sent and summed in bfloat16 or wider, within the bound.
A program may use at most 64 MiB of HBM per device.

v0:
```python
import math
import jax
import jax.numpy as jnp
from jax import lax
from jax.sharding import PartitionSpec as P

HEADS = 64
HD = 128
KV_HEADS = 8


def from_behind(block, axis, distance):
    devices = range(lax.axis_size(axis))
    route = [(i - distance, i) for i in devices if i - distance in devices]
    return lax.ppermute(block, axis, route)


def layout(image_counts, text_counts, tokens):
    lengths = (image_counts + text_counts).reshape(-1)
    images = image_counts.reshape(-1)
    ends = jnp.cumsum(lengths)
    starts = ends - lengths
    before = jnp.cumsum(images) - images
    position = jnp.arange(tokens, dtype=jnp.int32)
    request = jnp.sum((position[:, None] >= ends[None, :]).astype(jnp.int32), axis=1)
    member = request[:, None] == jnp.arange(lengths.shape[0], dtype=jnp.int32)[None, :]
    first = jnp.sum(jnp.where(member, starts[None, :], 0), axis=1)
    count = jnp.sum(jnp.where(member, images[None, :], 0), axis=1)
    earlier = jnp.sum(jnp.where(member, before[None, :], 0), axis=1)
    offset = position - first
    is_image = (offset >= 1) & (offset <= count)
    row_index = jnp.where(is_image, earlier + offset - 1, 0)
    return (request, is_image, row_index)


def pick_groups(gathered, first_group, local_groups):
    rows_here = gathered.shape[0]
    shaped = gathered.reshape(rows_here, HD, KV_HEADS)
    picked = lax.dynamic_slice_in_dim(shaped, first_group, local_groups, 2)
    return jnp.swapaxes(picked, 1, 2).reshape(rows_here, local_groups * HD)


def shards(
    text_embed,
    patch_hidden,
    merge_weight,
    merge_bias,
    norm_gain,
    query_weight,
    key_weight,
    value_weight,
    image_counts,
    text_counts,
):
    tokens, columns = text_embed.shape
    heads_here = columns // HD
    group_size = HEADS // KV_HEADS
    local_groups = max(1, heads_here // group_size)
    shared_heads = heads_here // local_groups
    first_group = lax.axis_index(("seq", "mp")) * heads_here // group_size
    bias_f = merge_bias.astype(jnp.float32)
    act = jax.nn.gelu(
        lax.all_gather(patch_hidden, ("seq", "mp"), axis=0, tiled=True).astype(jnp.float32),
        approximate=False,
    ).astype(jnp.bfloat16)
    section_rows = (jnp.dot(act, merge_weight, preferred_element_type=jnp.float32) + bias_f).astype(
        jnp.bfloat16
    )
    merged = lax.all_gather(section_rows, "section", axis=0, tiled=True)
    request, is_image, row_index = layout(image_counts, text_counts, tokens)
    start_state = jnp.where(is_image[:, None], jnp.take(merged, row_index, axis=0), text_embed)
    blocks = 2
    rows = tokens // blocks
    depth = lax.axis_size("section")
    section_here = lax.axis_index("section")
    gain = norm_gain[0].astype(jnp.float32)[None, :]
    position = jnp.arange(tokens, dtype=jnp.int32)
    key_cache = jnp.zeros((tokens, local_groups * HD), jnp.bfloat16)
    value_cache = jnp.zeros((tokens, local_groups * HD), jnp.bfloat16)
    hidden = jnp.zeros((tokens, columns), jnp.bfloat16)
    incoming = jnp.zeros((rows, columns), jnp.bfloat16)
    turns = blocks + depth - 1
    for tick in range(turns):
        block = tick - section_here
        valid = (block >= 0) & (block < blocks)
        first_row = jnp.clip(block, 0, blocks - 1) * rows
        if tick < blocks:
            fresh = start_state[tick * rows : (tick + 1) * rows]
            current = jnp.where(section_here == 0, fresh, incoming)
        else:
            current = incoming
        whole = lax.all_gather(current, ("seq", "mp"), axis=1, tiled=True)
        xf = whole.astype(jnp.float32)
        scale = lax.rsqrt(jnp.mean(xf * xf, axis=1, keepdims=True) + 1e-06)
        normed = (xf * scale * gain).astype(jnp.bfloat16)
        query = jnp.dot(normed, query_weight[0], preferred_element_type=jnp.float32).astype(
            jnp.bfloat16
        )
        key_part = jnp.dot(normed, key_weight[0], preferred_element_type=jnp.float32).astype(
            jnp.bfloat16
        )
        value_part = jnp.dot(normed, value_weight[0], preferred_element_type=jnp.float32).astype(
            jnp.bfloat16
        )
        key_all, value_all = (
            lax.all_gather(key_part, ("seq", "mp"), axis=1, tiled=True),
            lax.all_gather(value_part, ("seq", "mp"), axis=1, tiled=True),
        )
        key = pick_groups(key_all, first_group, local_groups)
        value = pick_groups(value_all, first_group, local_groups)
        key_cache = jnp.where(
            valid, lax.dynamic_update_slice_in_dim(key_cache, key, first_row, 0), key_cache
        )
        value_cache = jnp.where(
            valid, lax.dynamic_update_slice_in_dim(value_cache, value, first_row, 0), value_cache
        )
        query_request = lax.dynamic_slice_in_dim(request, first_row, rows)
        query_position = first_row + jnp.arange(rows, dtype=jnp.int32)
        allowed = (request[None, :] == query_request[:, None]) & (
            position[None, :] <= query_position[:, None]
        )
        scores = jnp.einsum(
            "qngd,knd->ngqk",
            query.reshape(rows, local_groups, shared_heads, HD),
            key_cache.reshape(tokens, local_groups, HD),
            preferred_element_type=jnp.float32,
        ) / math.sqrt(HD)
        scores = jnp.where(allowed[None, None, :, :], scores, -1e30)
        probs = jax.nn.softmax(scores, axis=-1).astype(jnp.bfloat16)
        attended = jnp.einsum(
            "ngqk,knd->qngd",
            probs,
            value_cache.reshape(tokens, local_groups, HD),
            preferred_element_type=jnp.float32,
        ).reshape(rows, columns)
        state = (current.astype(jnp.float32) + attended).astype(jnp.bfloat16)
        hidden = jnp.where(
            valid, lax.dynamic_update_slice_in_dim(hidden, state, first_row, 0), hidden
        )
        if tick + 1 < turns:
            incoming = from_behind(state, "section", 1)
    return hidden[None]


def solution(mesh):
    in_specs = (
        P(None, ("seq", "mp")),
        P(("section", "seq", "mp"), None),
        P(None, ("seq", "mp")),
        P(("seq", "mp")),
        P("section", None),
        P("section", None, ("seq", "mp")),
        P("section", None, ("seq", "mp")),
        P("section", None, ("seq", "mp")),
        P(),
        P(),
    )
    out_specs = P("section", None, ("seq", "mp"))
    return jax.shard_map(shards, mesh=mesh, in_specs=in_specs, out_specs=out_specs, check_vma=False)
```

profile of v0, /device:TPU:1, one launch (start us, length us, event | category | flops | bytes accessed | tf_op | source)
XLA Modules:
  0.0 1018.5 jit_solution(12970196134366100098)
XLA Ops:
  6.5 0.8 add.207
  9.1 55.3 %all-gather = bf16[64,1,5120]{2,1,0:T(2,128)(2,1)S(1)} all-gather(bf16[1,1,5120]{2,1,0:T(2,128)(2,1)} %bitcast.312), channel_id=1, replica_groups=mesh['section'=4,'seq'=32,'mp'=2] {'seq','mp'}, dimensions={0}, use_global_device_ids=true | all-gather | bytes 665600 | tf_op jit(solution)/shard_map/all_gather | solution.py:63
  64.3 1.4 broadcast_multiply_fusion
  65.7 2.4 convert_element_type.182
  68.8 4.7 fusion.80
  73.5 9.6 all_gather.52
  83.1 1.4 gather_fusion
  85.6 72.4 %all-gather.7.cloned.1.call-done = bf16[160,8192]{1,0:T(8,128)(2,1)} async-done(((bf16[160,128]{1,0:T(8,128)(2,1)}), bf16[160,8192]{1,0:T(8,128)(2,1)}) %all-gather.7.cloned.1.call-update) | async-done | bytes 2621456 | tf_op jit(solution)/shard_map/all_gather | solution.py:92
  158.0 2.5 fusion
  161.3 1.5 copy-done.5
  163.6 50.3 %all_gather.55 = bf16[160,1024]{0,1:T(8,128)(2,1)S(1)} all-gather(bf16[160,16]{0,1:T(8,128)(2,1)S(1)} %convolution_convert_fusion.8), channel_id=1, replica_groups=mesh['section'=4,'seq'=32,'mp'=2] {'seq','mp'}, dimensions={1}, use_global_device_ids=true | all-gather | bytes 332800 | tf_op jit(solution)/shard_map/all_gather | solution.py:106
  214.2 2.5 convolution_convert_fusion.9
  216.7 49.6 %all_gather.54 = bf16[160,1024]{0,1:T(8,128)(2,1)S(1)} all-gather(bf16[160,16]{0,1:T(8,128)(2,1)S(1)} %convolution_convert_fusion.9), channel_id=1, replica_groups=mesh['section'=4,'seq'=32,'mp'=2] {'seq','mp'}, dimensions={1}, use_global_device_ids=true | all-gather | bytes 332800 | tf_op jit(solution)/shard_map/all_gather | solution.py:107
  266.6 2.8 fusion.149
  270.0 3.1 collective-permute-start
  273.1 1.1 collective-permute-done
  274.9 71.6 %all-gather.9.cloned.1.call-done = bf16[160,8192]{1,0:T(8,128)(2,1)} async-done(((bf16[160,128]{1,0:T(8,128)(2,1)}), bf16[160,8192]{1,0:T(8,128)(2,1)}) %all-gather.9.cloned.1.call-update) | async-done | bytes 2621456 | tf_op jit(solution)/shard_map/all_gather | solution.py:92
  346.5 2.5 fusion.3
  349.8 0.8 convolution_convert_fusion.7
  350.6 0.8 convolution_convert_fusion.6
  351.4 50.5 %all_gather.57 = bf16[160,1024]{0,1:T(8,128)(2,1)S(1)} all-gather(bf16[160,16]{0,1:T(8,128)(2,1)S(1)} %convolution_convert_fusion.7), channel_id=1, replica_groups=mesh['section'=4,'seq'=32,'mp'=2] {'seq','mp'}, dimensions={1}, use_global_device_ids=true | all-gather | bytes 332800 | tf_op jit(solution)/shard_map/all_gather | solution.py:107
  402.1 49.6 %all_gather.58 = bf16[160,1024]{0,1:T(8,128)(2,1)S(1)} all-gather(bf16[160,16]{0,1:T(8,128)(2,1)S(1)} %convolution_convert_fusion.6), channel_id=1, replica_groups=mesh['section'=4,'seq'=32,'mp'=2] {'seq','mp'}, dimensions={1}, use_global_device_ids=true | all-gather | bytes 332800 | tf_op jit(solution)/shard_map/all_gather | solution.py:106
  452.1 2.8 fusion.152
  455.4 3.1 collective-permute-start.1
  458.5 1.1 collective-permute-done.1
  460.3 71.6 %all-gather.11.cloned.1.call-done = bf16[160,8192]{1,0:T(8,128)(2,1)} async-done(((bf16[160,128]{1,0:T(8,128)(2,1)}), bf16[160,8192]{1,0:T(8,128)(2,1)}) %all-gather.11.cloned.1.call-update) | async-done | bytes 2621456 | tf_op jit(solution)/shard_map/all_gather | solution.py:92
  531.9 2.5 fusion.6
  535.9 0.8 convolution_convert_fusion.5
  536.7 50.3 %all_gather.61 = bf16[160,1024]{0,1:T(8,128)(2,1)S(1)} all-gather(bf16[160,16]{0,1:T(8,128)(2,1)S(1)} %convolution_convert_fusion.4), channel_id=1, replica_groups=mesh['section'=4,'seq'=32,'mp'=2] {'seq','mp'}, dimensions={1}, use_global_device_ids=true | all-gather | bytes 332800 | tf_op jit(solution)/shard_map/all_gather | solution.py:106
  587.3 49.6 %all_gather.60 = bf16[160,1024]{0,1:T(8,128)(2,1)S(1)} all-gather(bf16[160,16]{0,1:T(8,128)(2,1)S(1)} %convolution_convert_fusion.5), channel_id=1, replica_groups=mesh['section'=4,'seq'=32,'mp'=2] {'seq','mp'}, dimensions={1}, use_global_device_ids=true | all-gather | bytes 332800 | tf_op jit(solution)/shard_map/all_gather | solution.py:107
  637.2 2.8 fusion.155
  640.6 3.1 collective-permute-start.2
  643.7 1.1 collective-permute-done.2
  645.5 71.6 %all-gather.13.cloned.1.call-done = bf16[160,8192]{1,0:T(8,128)(2,1)} async-done(((bf16[160,128]{1,0:T(8,128)(2,1)}), bf16[160,8192]{1,0:T(8,128)(2,1)}) %all-gather.13.cloned.1.call-update) | async-done | bytes 2621456 | tf_op jit(solution)/shard_map/all_gather | solution.py:92
  717.0 2.5 fusion.9
  721.1 0.8 convolution_convert_fusion.3
  721.9 50.3 %all_gather.64 = bf16[160,1024]{0,1:T(8,128)(2,1)S(1)} all-gather(bf16[160,16]{0,1:T(8,128)(2,1)S(1)} %convolution_convert_fusion.2), channel_id=1, replica_groups=mesh['section'=4,'seq'=32,'mp'=2] {'seq','mp'}, dimensions={1}, use_global_device_ids=true | all-gather | bytes 332800 | tf_op jit(solution)/shard_map/all_gather | solution.py:106
  772.5 49.6 %all_gather.63 = bf16[160,1024]{0,1:T(8,128)(2,1)S(1)} all-gather(bf16[160,16]{0,1:T(8,128)(2,1)S(1)} %convolution_convert_fusion.3), channel_id=1, replica_groups=mesh['section'=4,'seq'=32,'mp'=2] {'seq','mp'}, dimensions={1}, use_global_device_ids=true | all-gather | bytes 332800 | tf_op jit(solution)/shard_map/all_gather | solution.py:107
  822.4 2.8 fusion.158
  825.8 3.1 collective-permute-start.3
  828.9 1.1 collective-permute-done.3
  831.2 71.0 %all-gather.15.cloned.1.call-done = bf16[160,8192]{1,0:T(8,128)(2,1)} async-done(((bf16[160,128]{1,0:T(8,128)(2,1)}), bf16[160,8192]{1,0:T(8,128)(2,1)}) %all-gather.15.cloned.1.call-update) | async-done | bytes 2621456 | tf_op jit(solution)/shard_map/all_gather | solution.py:92
  902.2 2.5 fusion.12
  906.3 0.8 convolution_convert_fusion.1
  907.1 50.1 %all_gather.67 = bf16[160,1024]{0,1:T(8,128)(2,1)S(1)} all-gather(bf16[160,16]{0,1:T(8,128)(2,1)S(1)} %convolution_convert_fusion), channel_id=1, replica_groups=mesh['section'=4,'seq'=32,'mp'=2] {'seq','mp'}, dimensions={1}, use_global_device_ids=true | all-gather | bytes 332800 | tf_op jit(solution)/shard_map/all_gather | solution.py:106
  957.4 49.9 %all_gather.66 = bf16[160,1024]{0,1:T(8,128)(2,1)S(1)} all-gather(bf16[160,16]{0,1:T(8,128)(2,1)S(1)} %convolution_convert_fusion.1), channel_id=1, replica_groups=mesh['section'=4,'seq'=32,'mp'=2] {'seq','mp'}, dimensions={1}, use_global_device_ids=true | all-gather | bytes 332800 | tf_op jit(solution)/shard_map/all_gather | solution.py:107
  1007.6 2.8 fusion.161
  1010.7 0.9 fusion.109
  (137 shorter events, 18.5 us)
Async XLA Ops:
  6.5 260.1 %copy-start = (bf16[1,8192,128]{2,1,0:T(8,128)(2,1)S(1)}, bf16[1,8192,128]{2,1,0:T(8,128)(2,1)}, u32[]{:S(2)}) copy-start(bf16[1,8192,128]{2,1,0:T(8,128)(2,1)} %param.15) | copy-start | bytes 6291460
  6.5 151.5 %all-gather.7.cloned.1.call-start = ((), (), s32[]{:S(2)}) async-start(), calls=%async_computation | async-start | bytes 2662400 | tf_op jit(solution)/shard_map/all_gather | solution.py:92
  64.3 4.4 copy-start.23
  68.8 15.8 %copy-start.15 = (bf16[320,128]{1,0:T(8,128)(2,1)S(1)}, bf16[320,128]{1,0:T(8,128)(2,1)}, u32[]{:S(2)}) copy-start(bf16[320,128]{1,0:T(8,128)(2,1)} %param.10) | copy-start | bytes 245764
  68.8 16.7 %copy-start.22 = (bf16[1,8192]{1,0:T(2,128)(2,1)S(1)}, bf16[1,8192]{1,0:T(2,128)(2,1)}, u32[]{:S(2)}) copy-start(bf16[1,8192]{1,0:T(2,128)(2,1)} %param.14) | copy-start | bytes 49156
  85.4 261.2 %all-gather.9.cloned.1.call-start = ((), (), s32[]{:S(2)}) async-start(), calls=%async_computation.1 | async-start | bytes 2662400 | tf_op jit(solution)/shard_map/all_gather | solution.py:92
  158.0 2.5 copy-start.6
  160.6 2.2 copy-start.11
  161.3 1.5 copy-start.5
  162.8 51.4 %copy-start.12 = (bf16[1,8192,16]{1,2,0:T(8,128)(2,1)S(1)}, bf16[1,8192,16]{1,2,0:T(8,128)(2,1)}, u32[]{:S(2)}) copy-start(bf16[1,8192,16]{1,2,0:T(8,128)(2,1)} %param.17) | copy-start | bytes 786436
  266.6 3.1 copy-start.13
  270.0 4.2 collective-permute-start
  274.9 257.0 %all-gather.11.cloned.1.call-start = ((), (), s32[]{:S(2)}) async-start(), calls=%async_computation.2 | async-start | bytes 2662400 | tf_op jit(solution)/shard_map/all_gather | solution.py:92
  346.5 2.5 copy-start.8
  349.8 1.6 copy-start.2
  452.1 3.1 copy-start.14
  455.4 4.2 collective-permute-start.1
  459.6 0.6 copy-start.18
  460.2 256.8 %all-gather.13.cloned.1.call-start = ((), (), s32[]{:S(2)}) async-start(), calls=%async_computation.3 | async-start | bytes 2662400 | tf_op jit(solution)/shard_map/all_gather | solution.py:92
  531.9 2.5 copy-start.9
  535.1 1.6 copy-start.3
  637.2 3.1 copy-start.19
  640.6 4.2 collective-permute-start.2
  644.8 0.6 copy-start.20
  645.4 256.8 %all-gather.15.cloned.1.call-start = ((), (), s32[]{:S(2)}) async-start(), calls=%async_computation.4 | async-start | bytes 2662400 | tf_op jit(solution)/shard_map/all_gather | solution.py:92
  717.0 2.5 copy-start.10
  720.3 1.6 copy-start.4
  822.4 3.1 copy-start.21
  825.8 4.2 collective-permute-start.3
  830.0 0.6 copy-start.16
  902.2 2.5 copy-start.7
  905.5 1.6 copy-start.1
  1007.6 3.1 copy-start.17
Sparse Core Ops, SparseCore 0:
  85.5 72.5 all-gather.6
  275.0 71.4 all-gather.8
  460.4 71.4 all-gather.10
  645.5 71.4 all-gather.12
  830.7 71.4 all-gather.14
where the time goes:
time: 1030 us; the launch traced here: 1020 us
  blocking collectives  565 us (55%)
  waiting for transfers between devices  363 us (35%)
  matrix products  30.4 us (3%)
  other arithmetic  24.1 us (2%)
  between operations  14.2 us (1%)
  starting transfers between devices  12.5 us (1%)
    all_gather x5, waiting for transfers between devices, shards(): whole = lax.all_gather(current, ('seq', 'mp'), axis=1, tiled=True)  358 us
    all_gather x5, blocking collectives, shards(): lax.all_gather(key_part, ('seq', 'mp'), axis=1, tiled=True)  251 us
    all_gather x5, blocking collectives, shards(): lax.all_gather(value_part, ('seq', 'mp'), axis=1, tiled=True)  249 us
    all_gather x1, blocking collectives, shards(): lax.all_gather(patch_hidden, ('seq', 'mp'), axis=0, tiled=True)  55.3 us
  transfers between devices with their start and end apart: 9, of which 9 were waited for; matrix products, arithmetic and copies ran while one was open for 0% of the time, Pallas kernels for 0%

commit v1 on v0

--- a/solution.py
+++ b/solution.py
@@ -7,6 +7,12 @@
 HEADS = 64
 HD = 128
 KV_HEADS = 8
+
+
+def point_spot(mat):
+    x_next = jnp.stack([mat] * lax.axis_size(("seq", "mp")), axis=0)
+    aux = lax.all_to_all(x_next, ("seq", "mp"), split_axis=0, concat_axis=0)
+    return jnp.concatenate(aux, axis=1)
 
 
 def from_behind(block, axis, distance):
@@ -104,7 +110,7 @@
         )
         key_all, value_all = (
             lax.all_gather(key_part, ("seq", "mp"), axis=1, tiled=True),
-            lax.all_gather(value_part, ("seq", "mp"), axis=1, tiled=True),
+            point_spot(value_part),
         )
         key = pick_groups(key_all, first_group, local_groups)
         value = pick_groups(value_all, first_group, local_groups)

time: 1030 us -> 903 us (0.88)
  blocking collectives: 565 us -> 320 us
  waiting for transfers between devices: 363 us -> 419 us
  starting transfers between devices: 12.5 us -> 48.9 us
  local copies, waits for them, and re-layouts: 10 us -> 23.2 us
    all_gather x5 -> x0, blocking collectives: 249 us -> none  [shards(): lax.all_gather(value_part, ('seq', 'mp'), axis=1, tiled=True)]
    all_to_all x0 -> x5, waiting for transfers between devices: none -> 55.9 us  [point_spot(): aux = lax.all_to_all(x_next, ('seq', 'mp'), split_axis=0, concat_axis=0)]
    all_to_all x0 -> x5, starting transfers between devices: none -> 35.8 us  [point_spot(): aux = lax.all_to_all(x_next, ('seq', 'mp'), split_axis=0, concat_axis=0)]
  transfers between devices with their start and end apart: 9 -> 14, of which waited for: 9 -> 13; matrix products, arithmetic and copies ran while one was open for 0% -> 2% of each run, Pallas kernels for 0% -> 0%
where the time goes in v1:
time: 903 us; the launch traced here: 893 us
  waiting for transfers between devices  419 us (46%)
  blocking collectives  320 us (35%)
  starting transfers between devices  48.9 us (5%)
  matrix products  36 us (4%)
  other arithmetic  31.9 us (4%)
  local copies, waits for them, and re-layouts  23.2 us (3%)
  between operations  14.1 us (2%)
    all_gather x5, waiting for transfers between devices, shards(): whole = lax.all_gather(current, ('seq', 'mp'), axis=1, tiled=True)  359 us
    all_gather x5, blocking collectives, shards(): lax.all_gather(key_part, ('seq', 'mp'), axis=1, tiled=True)  255 us
    all_to_all x5, waiting for transfers between devices, point_spot(): aux = lax.all_to_all(x_next, ('seq', 'mp'), split_axis=0, concat_axis=0)  55.9 us
    all_gather x1, blocking collectives, shards(): lax.all_gather(patch_hidden, ('seq', 'mp'), axis=0, tiled=True)  55.3 us
    all_to_all x5, starting transfers between devices, point_spot(): aux = lax.all_to_all(x_next, ('seq', 'mp'), split_axis=0, concat_axis=0)  35.8 us
  transfers between devices with their start and end apart: 14, of which 13 were waited for; matrix products, arithmetic and copies ran while one was open for 2% of the time, Pallas kernels for 0%

profile of v1, /device:TPU:1, one launch (start us, length us, event | category | flops | bytes accessed | tf_op | source)
XLA Modules:
  0.0 892.8 jit_solution(811815168625584687)
XLA Ops:
  9.1 55.3 %all-gather = bf16[64,1,5120]{2,1,0:T(2,128)(2,1)S(1)} all-gather(bf16[1,1,5120]{2,1,0:T(2,128)(2,1)} %bitcast.322), channel_id=1, replica_groups=mesh['section'=4,'seq'=32,'mp'=2] {'seq','mp'}, dimensions={0}, use_global_device_ids=true | all-gather | bytes 665600 | tf_op jit(solution)/shard_map/all_gather | solution.py:69
  65.7 2.4 convert_element_type.182
  68.8 4.7 fusion.80
  73.5 9.6 %all_gather.37 = bf16[256,128]{1,0:T(8,128)(2,1)S(1)} all-gather(bf16[64,128]{1,0:T(8,128)(2,1)S(1)} %fusion.80), channel_id=1, replica_groups=mesh['section'=4,'seq'=32,'mp'=2] {'section'}, dimensions={0}, use_global_device_ids=true | all-gather | bytes 81920 | tf_op jit(solution)/shard_map/all_gather | solution.py:75
  83.1 1.4 gather_fusion
  86.8 71.9 %all-gather.7.cloned.1.call-done = bf16[160,8192]{1,0:T(8,128)(2,1)} async-done(((bf16[160,128]{1,0:T(8,128)(2,1)}), bf16[160,8192]{1,0:T(8,128)(2,1)}) %all-gather.7.cloned.1.call-update) | async-done | bytes 2621456 | tf_op jit(solution)/shard_map/all_gather | solution.py:98
  158.7 2.5 fusion
  162.0 1.5 copy-done.2
  164.2 50.3 %all_gather.39 = bf16[160,1024]{0,1:T(8,128)(2,1)S(1)} all-gather(bf16[160,16]{0,1:T(8,128)(2,1)S(1)} %convolution_convert_fusion.8), channel_id=1, replica_groups=mesh['section'=4,'seq'=32,'mp'=2] {'seq','mp'}, dimensions={1}, use_global_device_ids=true | all-gather | bytes 332800 | tf_op jit(solution)/shard_map/all_gather | solution.py:112
  214.8 2.5 convolution_convert_fusion.9
  218.2 6.9 all-to-all-start
  225.2 2.8 fusion.149
  228.9 13.9 %all-to-all-done = bf16[64,160,16]{1,2,0:T(8,128)(2,1)S(1)} async-done(((bf16[64,160,16]{1,2,0:T(8,128)(2,1)}), bf16[64,160,16]{1,2,0:T(8,128)(2,1)S(1)}, u32[]{:S(2)}, u32[]{:S(2)}) %all-to-all-start) | async-done | bytes 327712 | tf_op jit(solution)/shard_map/all_to_all | solution.py:14
  245.8 3.1 collective-permute-start
  249.9 1.4 slice_select_fusion
  251.4 71.6 %all-gather.9.cloned.1.call-done = bf16[160,8192]{1,0:T(8,128)(2,1)} async-done(((bf16[160,128]{1,0:T(8,128)(2,1)}), bf16[160,8192]{1,0:T(8,128)(2,1)}) %all-gather.9.cloned.1.call-update) | async-done | bytes 2621456 | tf_op jit(solution)/shard_map/all_gather | solution.py:98
  323.0 2.5 fusion.3
  326.2 1.5 copy-done.1
  329.4 8.0 all-to-all-start.1
  338.0 2.5 convolution_convert_fusion.6
  340.6 54.5 %all_gather.41 = bf16[160,1024]{0,1:T(8,128)(2,1)S(1)} all-gather(bf16[160,16]{0,1:T(8,128)(2,1)S(1)} %convolution_convert_fusion.6), channel_id=1, replica_groups=mesh['section'=4,'seq'=32,'mp'=2] {'seq','mp'}, dimensions={1}, use_global_device_ids=true | all-gather | bytes 332800 | tf_op jit(solution)/shard_map/all_gather | solution.py:112
  397.1 2.9 fusion.152
  400.5 3.1 collective-permute-start.1
  405.9 74.2 %all-gather.11.cloned.1.call-done = bf16[160,8192]{1,0:T(8,128)(2,1)} async-done(((bf16[160,128]{1,0:T(8,128)(2,1)}), bf16[160,8192]{1,0:T(8,128)(2,1)}) %all-gather.11.cloned.1.call-update) | async-done | bytes 2621456 | tf_op jit(solution)/shard_map/all_gather | solution.py:98
  480.0 2.5 fusion.6
  484.9 50.1 %all_gather.43 = bf16[160,1024]{0,1:T(8,128)(2,1)S(1)} all-gather(bf16[160,16]{0,1:T(8,128)(2,1)S(1)} %convolution_convert_fusion.4), channel_id=1, replica_groups=mesh['section'=4,'seq'=32,'mp'=2] {'seq','mp'}, dimensions={1}, use_global_device_ids=true | all-gather | bytes 332800 | tf_op jit(solution)/shard_map/all_gather | solution.py:112
  536.1 6.9 all-to-all-start.2
  543.5 2.8 fusion.155
  547.2 13.5 %all-to-all-done.2 = bf16[64,160,16]{1,2,0:T(8,128)(2,1)S(1)} async-done(((bf16[64,160,16]{1,2,0:T(8,128)(2,1)}), bf16[64,160,16]{1,2,0:T(8,128)(2,1)S(1)}, u32[]{:S(2)}, u32[]{:S(2)}) %all-to-all-start.2) | async-done | bytes 327712 | tf_op jit(solution)/shard_map/all_to_all | solution.py:14
  562.5 1.4 fusion.115
  564.0 1.7 select_dynamic-update-slice_fusion.1
  565.7 3.1 collective-permute-start.2
  571.1 71.0 %all-gather.13.cloned.1.call-done = bf16[160,8192]{1,0:T(8,128)(2,1)} async-done(((bf16[160,128]{1,0:T(8,128)(2,1)}), bf16[160,8192]{1,0:T(8,128)(2,1)}) %all-gather.13.cloned.1.call-update) | async-done | bytes 2621456 | tf_op jit(solution)/shard_map/all_gather | solution.py:98
  642.1 2.5 fusion.9
  646.9 50.1 %all_gather.45 = bf16[160,1024]{0,1:T(8,128)(2,1)S(1)} all-gather(bf16[160,16]{0,1:T(8,128)(2,1)S(1)} %convolution_convert_fusion.2), channel_id=1, replica_groups=mesh['section'=4,'seq'=32,'mp'=2] {'seq','mp'}, dimensions={1}, use_global_device_ids=true | all-gather | bytes 332800 | tf_op jit(solution)/shard_map/all_gather | solution.py:112
  698.2 6.9 all-to-all-start.3
  705.2 2.8 fusion.158
  708.8 14.0 %all-to-all-done.3 = bf16[64,160,16]{1,2,0:T(8,128)(2,1)S(1)} async-done(((bf16[64,160,16]{1,2,0:T(8,128)(2,1)}), bf16[64,160,16]{1,2,0:T(8,128)(2,1)S(1)}, u32[]{:S(2)}, u32[]{:S(2)}) %all-to-all-start.3) | async-done | bytes 327712 | tf_op jit(solution)/shard_map/all_to_all | solution.py:14
  724.6 1.4 fusion.113
  726.0 1.7 select_dynamic-update-slice_fusion
  727.8 3.3 collective-permute-start.3
  732.6 1.5 copy.84
  734.1 70.0 %all-gather.15.cloned.1.call-done = bf16[160,8192]{1,0:T(8,128)(2,1)} async-done(((bf16[160,128]{1,0:T(8,128)(2,1)}), bf16[160,8192]{1,0:T(8,128)(2,1)}) %all-gather.15.cloned.1.call-update) | async-done | bytes 2621456 | tf_op jit(solution)/shard_map/all_gather | solution.py:98
  804.2 2.5 fusion.12
  809.0 50.1 %all_gather.47 = bf16[160,1024]{0,1:T(8,128)(2,1)S(1)} all-gather(bf16[160,16]{0,1:T(8,128)(2,1)S(1)} %convolution_convert_fusion), channel_id=1, replica_groups=mesh['section'=4,'seq'=32,'mp'=2] {'seq','mp'}, dimensions={1}, use_global_device_ids=true | all-gather | bytes 332800 | tf_op jit(solution)/shard_map/all_gather | solution.py:112
  860.2 6.9 all-to-all-start.4
  867.2 2.9 fusion.161
  870.3 14.5 %all-to-all-done.4 = bf16[64,160,16]{1,2,0:T(8,128)(2,1)S(1)} async-done(((bf16[64,160,16]{1,2,0:T(8,128)(2,1)}), bf16[64,160,16]{1,2,0:T(8,128)(2,1)S(1)}, u32[]{:S(2)}, u32[]{:S(2)}) %all-to-all-start.4) | async-done | bytes 327712 | tf_op jit(solution)/shard_map/all_to_all | solution.py:14
  (163 shorter events, 43.3 us)
Async XLA Ops:
  6.5 218.7 %copy-start = (bf16[1,8192,128]{2,1,0:T(8,128)(2,1)S(1)}, bf16[1,8192,128]{2,1,0:T(8,128)(2,1)}, u32[]{:S(2)}) copy-start(bf16[1,8192,128]{2,1,0:T(8,128)(2,1)} %param.15) | copy-start | bytes 6291460
  6.5 152.2 %all-gather.7.cloned.1.call-start = ((), (), s32[]{:S(2)}) async-start(), calls=%async_computation.5 | async-start | bytes 2662400 | tf_op jit(solution)/shard_map/all_gather | solution.py:98
  64.3 4.4 copy-start.31
  68.4 156.8 %copy-start.18 = (s32[320]{0:T(512)}, s32[320]{0:T(512)S(1)}, u32[]{:S(2)}) copy-start(s32[320]{0:T(512)S(1)} %convert_reduce_fusion) | copy-start | bytes 3844
  68.8 15.8 %copy-start.21 = (bf16[320,128]{1,0:T(8,128)(2,1)S(1)}, bf16[320,128]{1,0:T(8,128)(2,1)}, u32[]{:S(2)}) copy-start(bf16[320,128]{1,0:T(8,128)(2,1)} %param.10) | copy-start | bytes 245764
  68.8 17.3 %copy-start.28 = (bf16[1,8192]{1,0:T(2,128)(2,1)S(1)}, bf16[1,8192]{1,0:T(2,128)(2,1)}, u32[]{:S(2)}) copy-start(bf16[1,8192]{1,0:T(2,128)(2,1)} %param.14) | copy-start | bytes 49156
  84.7 0.6 copy-start.17
  158.7 2.5 copy-start.6
  161.2 2.2 copy-start.11
  161.9 1.5 copy-start.2
  163.5 51.3 %copy-start.12 = (bf16[1,8192,16]{1,2,0:T(8,128)(2,1)S(1)}, bf16[1,8192,16]{1,2,0:T(8,128)(2,1)}, u32[]{:S(2)}) copy-start(bf16[1,8192,16]{1,2,0:T(8,128)(2,1)} %param.17) | copy-start | bytes 786436
  218.2 24.6 %all-to-all-start = ((bf16[64,160,16]{1,2,0:T(8,128)(2,1)}), bf16[64,160,16]{1,2,0:T(8,128)(2,1)S(1)}, u32[]{:S(2)}, u32[]{:S(2)}) async-start(bf16[64,160,16]{1,2,0:T(8,128)(2,1)} %stack.10), calls=%async_computation | async-start | bytes 1048576 | tf_op jit(solution)/shard_map/all_to_all | solution.py:14
  225.1 97.8 %all-gather.9.cloned.1.call-start = ((), (), s32[]{:S(2)}) async-start(), calls=%async_computation.6 | async-start | bytes 2662400 | tf_op jit(solution)/shard_map/all_gather | solution.py:98
  228.1 16.6 %copy-start.29 = (f32[160]{0:T(256)}, f32[160]{0:T(256)S(1)}, u32[]{:S(2)}) copy-start(f32[160]{0:T(256)S(1)} %get-tuple-element.21) | copy-start | bytes 1924
  245.8 4.2 collective-permute-start
  323.0 2.5 copy-start.10
  326.2 1.5 copy-start.1
  329.4 66.6 %all-to-all-start.1 = ((bf16[64,160,16]{1,2,0:T(8,128)(2,1)}), bf16[64,160,16]{1,2,0:T(8,128)(2,1)S(1)}, u32[]{:S(2)}, u32[]{:S(2)}) async-start(bf16[64,160,16]{1,2,0:T(8,128)(2,1)} %stack.11), calls=%async_computation.1 | async-start | bytes 1048576 | tf_op jit(solution)/shard_map/all_to_all | solution.py:14
  337.4 142.6 %all-gather.11.cloned.1.call-start = ((), (), s32[]{:S(2)}) async-start(), calls=%async_computation.7 | async-start | bytes 2662400 | tf_op jit(solution)/shard_map/all_gather | solution.py:98
  397.1 3.1 copy-start.13
  397.1 3.1 copy-start.20
  400.5 82.8 %copy-start.15 = (bf16[320,128]{1,0:T(8,128)(2,1)}, bf16[320,128]{1,0:T(8,128)(2,1)S(1)}, u32[]{:S(2)}) copy-start(bf16[320,128]{1,0:T(8,128)(2,1)S(1)} %get-tuple-element.12) | copy-start | bytes 245764
  400.5 4.2 collective-permute-start.1
  404.7 0.6 copy-start.24
  480.0 2.5 copy-start.8
  483.3 1.6 copy-start.4
  484.1 59.4 %copy-start.19 = (s32[320]{0:T(512)S(1)}, s32[320]{0:T(512)}, u32[]{:S(2)}) copy-start(s32[320]{0:T(512)} %copy-done.18) | copy-start | bytes 3844
  536.1 24.6 %all-to-all-start.2 = ((bf16[64,160,16]{1,2,0:T(8,128)(2,1)}), bf16[64,160,16]{1,2,0:T(8,128)(2,1)S(1)}, u32[]{:S(2)}, u32[]{:S(2)}) async-start(bf16[64,160,16]{1,2,0:T(8,128)(2,1)} %stack.12), calls=%async_computation.2 | async-start | bytes 1048576 | tf_op jit(solution)/shard_map/all_to_all | solution.py:14
  543.0 99.1 %all-gather.13.cloned.1.call-start = ((), (), s32[]{:S(2)}) async-start(), calls=%async_computation.8 | async-start | bytes 2662400 | tf_op jit(solution)/shard_map/all_gather | solution.py:98
  543.5 20.4 %copy-start.25 = (bf16[160,128]{1,0:T(8,128)(2,1)S(1)}, bf16[160,128]{1,0:T(8,128)(2,1)}, u32[]{:S(2)}) copy-start(bf16[160,128]{1,0:T(8,128)(2,1)} %copy-done.24) | copy-start | bytes 122884
  565.7 4.2 collective-permute-start.2
  569.9 0.6 copy-start.26
  642.1 2.5 copy-start.9
  645.4 1.6 copy-start.5
  698.2 24.6 %all-to-all-start.3 = ((bf16[64,160,16]{1,2,0:T(8,128)(2,1)}), bf16[64,160,16]{1,2,0:T(8,128)(2,1)S(1)}, u32[]{:S(2)}, u32[]{:S(2)}) async-start(bf16[64,160,16]{1,2,0:T(8,128)(2,1)} %stack.13), calls=%async_computation.3 | async-start | bytes 1048576 | tf_op jit(solution)/shard_map/all_to_all | solution.py:14
  705.1 99.1 %all-gather.15.cloned.1.call-start = ((), (), s32[]{:S(2)}) async-start(), calls=%async_computation.9 | async-start | bytes 2662400 | tf_op jit(solution)/shard_map/all_gather | solution.py:98
  705.2 20.8 %copy-start.27 = (bf16[160,128]{1,0:T(8,128)(2,1)S(1)}, bf16[160,128]{1,0:T(8,128)(2,1)}, u32[]{:S(2)}) copy-start(bf16[160,128]{1,0:T(8,128)(2,1)} %copy-done.26) | copy-start | bytes 122884
  727.8 4.2 collective-permute-start.3
  731.9 0.6 copy-start.22
  804.2 2.5 copy-start.7
  807.4 1.6 copy-start.3
  808.2 59.0 %copy-start.30 = (s32[160]{0:T(256)S(1)}, s32[160]{0:T(256)}, u32[]{:S(2)}) copy-start(s32[160]{0:T(256)} %get-tuple-element.16) | copy-start | bytes 1924
  860.2 24.6 %all-to-all-start.4 = ((bf16[64,160,16]{1,2,0:T(8,128)(2,1)}), bf16[64,160,16]{1,2,0:T(8,128)(2,1)S(1)}, u32[]{:S(2)}, u32[]{:S(2)}) async-start(bf16[64,160,16]{1,2,0:T(8,128)(2,1)} %stack.14), calls=%async_computation.4 | async-start | bytes 1048576 | tf_op jit(solution)/shard_map/all_to_all | solution.py:14
  867.2 17.9 %copy-start.14 = (bf16[320,128]{1,0:T(8,128)(2,1)S(1)}, bf16[320,128]{1,0:T(8,128)(2,1)}, u32[]{:S(2)}) copy-start(bf16[320,128]{1,0:T(8,128)(2,1)} %fusion.113) | copy-start | bytes 245764
  867.2 18.0 %copy-start.16 = (bf16[320,128]{1,0:T(8,128)(2,1)S(1)}, bf16[320,128]{1,0:T(8,128)(2,1)}, u32[]{:S(2)}) copy-start(bf16[320,128]{1,0:T(8,128)(2,1)} %get-tuple-element.8) | copy-start | bytes 245764
  867.2 18.0 %copy-start.23 = (bf16[160,128]{1,0:T(8,128)(2,1)S(1)}, bf16[160,128]{1,0:T(8,128)(2,1)}, u32[]{:S(2)}) copy-start(bf16[160,128]{1,0:T(8,128)(2,1)} %copy-done.22) | copy-start | bytes 122884
Sparse Core Ops, SparseCore 0:
  86.1 72.5 all-gather.6
  251.5 71.4 all-gather.8
  405.4 74.5 all-gather.10
  570.6 71.4 all-gather.12
  732.7 71.4 all-gather.14
